TPU v7x, 128 devices: a whole 4x4x4 slice. The times are simulated.
128 devices in a mesh: wide: 8 (over z, core), narrow: 16 (over x, y).
Axes of the slice: x: 4, y: 4, z: 4, core: 2. Of those that a mesh axis runs over, the one named last changes fastest.
Arguments:
- vectors: float32 [131072, 1024], P(('wide', 'narrow'))
- pivots: int32 [256], replicated, may hold values from 0 to 131071, as said below
- integrals: float32 [131072, 256], P(('wide', 'narrow')), as said below
- destination: int32 [131072], P(('wide', 'narrow')), may hold values from 0 to 131071, as said below
Outputs:
- new_vectors: float32 [131072, 256], P(('wide', 'narrow'))
Inputs may be any that keep to these rules, and one draw needn't show every extreme that they name: `pivots`: 256 distinct pair rows, the first and the last pair row among them. Every pair row is the destination of exactly one slot. Rows 1024 * d to 1024 * (d + 1) - 1 belong to the device of index d along wide+narrow; of the slots of one device, at most 16 belong to the rows of one device, and some device sends exactly 16 to some device. `integrals`: the pivot block of the residual is symmetric and positive definite.
All inputs are finite; a program needn't handle non-finite values.
Results may differ from a plain program's by a relative error of at most 0.000084.
Values sent between devices are 32-bit elements; how exact they have to be, the bound alone decides.
A program may use at most 64 MiB of HBM per device.

v0:
```python
import random

import jax, jax.numpy as jnp
from jax import lax
from jax.experimental import pallas as pl
from jax.experimental.pallas import tpu as pltpu
from jax.sharding import PartitionSpec as P

F32, BF16, I32 = jnp.float32, jnp.bfloat16, jnp.int32
HI = lax.Precision.HIGHEST
NT = (((1,), (1,)), ((), ()))
NN = (((1,), (0,)), ((), ()))
TN = (((0,), (0,)), ((), ()))
BLOCK = 64
PAIRS = 131072
ROWS_DEV = 1024
VECS = 1024
PIVOTS = 256
CAP = 16
DEVICES = PAIRS // ROWS_DEV
CHIPS = DEVICES // 2
WIDE_NARROW = ("wide", "narrow")


def dot_hi(a, b, dims=(((1,), (0,)), ((), ()))):
    return lax.dot_general(a, b, dims, precision=HI, preferred_element_type=F32)

def factor_block(s, at):
    rows = lax.broadcasted_iota(I32, (BLOCK, 2 * BLOCK), 0)
    lanes = lax.broadcasted_iota(I32, (BLOCK, 2 * BLOCK), 1)
    other = BLOCK - at
    inside = (lanes >= at) & (lanes < at + BLOCK)
    t = jnp.where(inside, s, (rows == lanes - other).astype(F32))
    done = []
    for j in range(0, BLOCK, 2):
        top = j // 8 * 8
        i = j - top
        r0, r1 = t[i : i + 1, :], t[i + 1 : i + 2, :]
        c0 = jnp.broadcast_to(t[:, at + j : at + j + 1], t.shape)
        c1 = jnp.broadcast_to(t[:, at + j + 1 : at + j + 2], t.shape)
        a, b, c = c0[i : i + 1, :], c0[i + 1 : i + 2, :], c1[i + 1 : i + 2, :]
        inv = 1.0 / (a * c - b * b)
        u0 = (c * inv) * r0 - (b * inv) * r1
        u1 = (a * inv) * r1 - (b * inv) * r0
        ia = 1.0 / a
        done.append(r0 * lax.rsqrt(a))
        done.append((r1 - (b * ia) * r0) * lax.rsqrt(c - b * (b * ia)))
        below = lax.broadcasted_iota(I32, t.shape, 0) > i + 1
        t = jnp.where(below, t - c0 * u0 - c1 * u1, t)
        if (j + 2) % 8 == 0:
            t = t[8:, :]
    full = jnp.concatenate(done, axis=0)
    return full[:, other : other + BLOCK]

def invert_factor(a_ref, w_ref):
    n = a_ref.shape[0]
    w_ref[...] = jnp.zeros_like(w_ref)
    for k in range(0, n, BLOCK):
        e = k + BLOCK
        base = k // 128 * 128
        inv = factor_block(a_ref[k:e, base : base + 128], k - base)
        if k == 0:
            wk = inv
        else:
            wk = jnp.concatenate([dot_hi(inv, w_ref[k:e, :k]), inv], axis=1)
        w_ref[k:e, :e] = wk
        if e < n:
            col = dot_hi(a_ref[e:, k:e], inv, NT)
            a_ref[e:, e:] = a_ref[e:, e:] - dot_hi(col, col, NT)
            w_ref[e:, :e] = w_ref[e:, :e] - dot_hi(col, wk)


def dot_bf(a, b, dims=NN):
    return lax.dot_general(a, b, dims, preferred_element_type=F32)


def bf(x):
    return x.astype(F32).astype(BF16)


def split3(x):
    hi = x.astype(BF16)
    rest = x - hi.astype(F32)
    mid = rest.astype(BF16)
    return hi, mid, (rest - mid.astype(F32)).astype(BF16)


def dot3(a, b, dims):
    ah = a.astype(BF16)
    al = (a - ah.astype(F32)).astype(BF16)
    bh = b.astype(BF16)
    bl = (b - bh.astype(F32)).astype(BF16)
    return dot_bf(ah, bh, dims) + (dot_bf(ah, bl, dims) + dot_bf(al, bh, dims))


def column(row):
    return jnp.broadcast_to(row.astype(F32), (128, row.shape[1])).T.astype(I32)


def own_pivot_integrals(piv, dest, ints_ref, pint_ref):
    piv_col = column(piv)
    match = bf(
        jnp.concatenate([piv_col == dest[:, i : i + 128] for i in range(0, ROWS_DEV, 128)], axis=1)
    )
    rows = sum(dot_bf(match, part) for part in split3(ints_ref[...]))
    for ct in range(PIVOTS // 128):
        pint_ref[ct * 32 : ct * 32 + 32] = rows[:, ct * 128 : ct * 128 + 128].reshape(32, 8, 128)


def own_pivot_vectors(piv_smem, first, vec_ref, pvec_ref):
    def pick(t, _):
        for u in range(8):
            row = piv_smem[t * 8 + u] - first
            mine = (row >= 0) & (row < ROWS_DEV)
            values = vec_ref[pl.ds(jnp.where(mine, row, ROWS_DEV), 1), :]
            for ct in range(VECS // 128):
                pvec_ref[t // 16, ct // 2 * 16 + t % 16, ct % 2, u : u + 1, :] = values[
                    :, ct * 128 : ct * 128 + 128
                ]
        return 0

    lax.fori_loop(0, PIVOTS // 8, pick, 0)


def slot_maps(dest):
    owner = dest // ROWS_DEV
    local1 = dest - owner * ROWS_DEV + 1
    onehot = lax.broadcasted_iota(I32, (DEVICES, ROWS_DEV), 0) == owner
    onehot_bf = bf(onehot)
    before = bf(lax.broadcasted_iota(I32, (128, 128), 0) < lax.broadcasted_iota(I32, (128, 128), 1))
    ranks = []
    carry = jnp.zeros((DEVICES, 1), F32)
    for i in range(0, ROWS_DEV, 128):
        hot = onehot[:, i : i + 128]
        count = dot_bf(onehot_bf[:, i : i + 128], before) + carry
        ranks.append(jnp.sum(jnp.where(hot, count, 0.0), axis=0, keepdims=True))
        carry = carry + jnp.sum(hot.astype(F32), axis=1, keepdims=True)
    rank = jnp.concatenate(ranks, axis=1).astype(I32)
    slot = lax.broadcasted_iota(I32, (CAP, ROWS_DEV), 1)
    hit = lax.broadcasted_iota(I32, (CAP, ROWS_DEV), 0) == rank
    source = dot_bf(bf(jnp.where(hit, slot // 32, 0)), onehot_bf, NT) * 32.0
    source = source + dot_bf(bf(jnp.where(hit, slot % 32, 0)), onehot_bf, NT)
    hit = lax.broadcasted_iota(I32, (128, ROWS_DEV), 0) == rank
    target = dot_bf(onehot_bf, bf(jnp.where(hit, local1 // 32, 0)), NT) * 32.0
    target = target + dot_bf(onehot_bf, bf(jnp.where(hit, local1 % 32, 0)), NT)
    return jnp.clip(source.astype(I32), 0, ROWS_DEV - 1), target.astype(I32)


def row_places(target):
    by_slot = target.astype(F32).T.astype(I32)
    line = lax.broadcasted_iota(I32, (128, DEVICES), 0)
    block = lax.broadcasted_iota(I32, (128, DEVICES), 1)
    highs, blocks, slots = [], [], []
    for k in range(CAP):
        t = by_slot[k : k + 1, :] - 1
        highs.append(bf(line[:32] == t // 32))
        low = line == t % 32
        blocks.append(bf(jnp.where(low, block, 0)))
        slots.append(bf(jnp.where(low, k, 0)))
    high = jnp.concatenate(highs, axis=1)
    place = dot_bf(high, jnp.concatenate(blocks, axis=1), NT) * CAP
    place = place + dot_bf(high, jnp.concatenate(slots, axis=1), NT)
    return jnp.clip(place.astype(I32), 0, DEVICES * CAP - 1)


def far_first(offsets):
    offsets = list(offsets)
    random.Random(7).shuffle(offsets)
    return sorted(offsets, key=lambda o: -sum(min(v, 4 - v) for v in o[:3]))


CHIP_STEPS = far_first((z, x, y) for z in range(4) for x in range(4) for y in range(4) if (z, x, y) != (0, 0, 0))
ALL_STEPS = far_first(
    (z, x, y, c)
    for z in range(4) for x in range(4) for y in range(4) for c in range(2)
    if (z, x, y, c) != (0, 0, 0, 0)
)


def main_kernel(
    piv_smem, piv_ref, dest_ref, ints_hbm, vec_hbm, out_hbm,
    ints_ref, vec_ref, pvec_ref, pint_ref, from_ref, from_smem, send_ref, tgt_ref, rtgt_ref,
    pair_v, pair_i, mine, part, tile, all0, all1, a_ref, w_ref, prod_ref,
    recv_ref, place_ref, place_smem, rows_ref, out_ref, ssem, rsem, lsem, osem,
):
    wide, narrow = lax.axis_index("wide"), lax.axis_index("narrow")
    z, core, x, y = wide // 2, wide % 2, narrow // 4, narrow % 4
    chip = z * 16 + x * 4 + y
    me = wide * 16 + narrow

    def at(dz, dx, dy, dc=0):
        oz, ox, oy, oc = (z + dz) % 4, (x + dx) % 4, (y + dy) % 4, (core + dc) % 2
        return {"wide": oz * 2 + oc, "narrow": ox * 4 + oy}, oz * 16 + ox * 4 + oy

    def send(src, dst, stage, where):
        pltpu.make_async_remote_copy(
            src_ref=src, dst_ref=dst, send_sem=ssem.at[stage], recv_sem=rsem.at[stage],
            device_id=where, device_id_type=pl.DeviceIdType.MESH,
        ).start()

    def arrived(ref, stage):
        pltpu.make_async_copy(ref, ref, rsem.at[stage]).wait()

    def left(ref, stage):
        pltpu.make_async_copy(ref, ref, ssem.at[stage]).wait()

    load_vec = pltpu.make_async_copy(vec_hbm, vec_ref.at[pl.ds(0, ROWS_DEV)], lsem.at[0])
    load_vec.start()
    load_ints = pltpu.make_async_copy(ints_hbm, ints_ref, lsem.at[1])
    load_ints.start()
    barrier = pltpu.get_barrier_semaphore()
    for step in ALL_STEPS:
        pl.semaphore_signal(barrier, inc=1, device_id=at(*step)[0], device_id_type=pl.DeviceIdType.MESH)
    vec_ref[pl.ds(ROWS_DEV, 8), :] = jnp.zeros((8, VECS), F32)
    dest = dest_ref[...]
    load_ints.wait()
    own_pivot_integrals(piv_ref[...], dest, ints_ref, pint_ref)
    load_vec.wait()
    own_pivot_vectors(piv_smem, me * ROWS_DEV, vec_ref, pvec_ref)
    pl.semaphore_wait(barrier, DEVICES - 1)

    sibling = at(0, 0, 0, 1)[0]
    send(pvec_ref.at[1 - core], pair_v, 0, sibling)

    @pl.when(core == 1)
    def _():
        send(pint_ref, pair_i, 1, sibling)

    source, target = slot_maps(dest)
    from_ref[...] = source
    tgt_ref[...] = target.reshape(DEVICES, 1, 128)
    to_smem = pltpu.make_async_copy(from_ref, from_smem, lsem.at[2])
    to_smem.start()

    arrived(pair_v, 0)
    mine[:, 0:2] = pvec_ref[core] + pair_v[...]

    @pl.when(core == 0)
    def _():
        arrived(pair_i, 1)
        mine[:, 2] = pint_ref[...] + pair_i[...]
        for i, step in enumerate(CHIP_STEPS):
            where, home = at(*step)
            send(mine.at[home], part.at[i], 2, where)

    two = pl.ds(0, 2)

    @pl.when(core == 1)
    def _():
        for i, step in enumerate(CHIP_STEPS):
            where, home = at(*step)
            send(mine.at[home, two], part.at[i, two], 2, where)

    to_smem.wait()

    def pack(d, _):
        for k in range(CAP):
            send_ref[d, k : k + 1, :] = ints_ref[
                pl.ds(jnp.clip(from_smem[k, d], 0, ROWS_DEV - 1), 1), :
            ]
        return 0

    lax.fori_loop(0, DEVICES, pack, 0)
    others = pl.ds(0, CHIPS - 1)

    @pl.when(core == 0)
    def _():
        arrived(part, 2)
        tile[...] = jnp.sum(part[...], axis=0) + mine[chip]
        for step in CHIP_STEPS:
            send(tile, all0.at[chip], 4, at(*step)[0])
        all0[chip] = tile[...]

    @pl.when(core == 1)
    def _():
        arrived(all1.at[others], 2)
        tile[0:2] = jnp.sum(part[:, 0:2], axis=0) + mine[chip, 0:2]
        for step in CHIP_STEPS:
            send(tile.at[two], all1.at[chip], 4, at(*step)[0])
        all1[chip] = tile[0:2]

    steps = [at(*step)[0] for step in ALL_STEPS]
    for i, where in enumerate(steps):
        send(tgt_ref.at[where["wide"] * 16 + where["narrow"]], rtgt_ref.at[i], 9, where)
    rtgt_ref[DEVICES - 1] = tgt_ref[me]
    recv_ref[(DEVICES - 1) * CAP :, :] = send_ref[me]

    @pl.when(core == 0)
    def _():
        arrived(all0.at[others], 4)
        send(all0, all0, 6, sibling)

    @pl.when(core == 1)
    def _():
        arrived(all1.at[others], 4)
        send(all1, all1, 6, sibling)

    for i, where in enumerate(steps):
        send(
            send_ref.at[where["wide"] * 16 + where["narrow"]],
            recv_ref.at[pl.ds(i * CAP, CAP)], 8, where,
        )

    @pl.when(core == 0)
    def _():
        arrived(all1, 6)

    @pl.when(core == 1)
    def _():
        arrived(all0, 6)

    def pivot_columns(ct):
        top, end = ct * 16, ct * 16 + 16
        return jnp.concatenate(
            [
                jnp.concatenate(
                    [all0[top:end, u].reshape(128, 128), all1[top:end, u].reshape(128, 128)], axis=0
                )
                for u in range(2)
            ],
            axis=1,
        )

    block = jnp.concatenate([all0[u * 32 : u * 32 + 32, 2].reshape(PIVOTS, 128) for u in range(2)], axis=1)
    for ct in range(VECS // 256):
        cols = pivot_columns(ct)
        block = block - dot_hi(cols, cols, NT)
    a_ref[...] = (block + block.T) * 0.5
    invert_factor(a_ref, w_ref)
    prod_ref[...] = sum(
        dot3(vec_ref[:ROWS_DEV, ct * 256 : ct * 256 + 256], pivot_columns(ct), NT)
        for ct in range(VECS // 256)
    )
    arrived(rtgt_ref.at[pl.ds(0, DEVICES - 1)], 9)
    place_ref[...] = row_places(rtgt_ref[...].reshape(DEVICES, 128))
    place_copy = pltpu.make_async_copy(place_ref, place_smem, lsem.at[3])
    place_copy.start()
    place_copy.wait()
    arrived(recv_ref.at[pl.ds(0, (DEVICES - 1) * CAP)], 8)
    outs = []
    for q in range(4):
        top = q * 256

        def take(t, _, q=q):
            for u in range(32):
                place = jnp.clip(place_smem[q * 8 + t, u], 0, DEVICES * CAP - 1)
                rows_ref[t * 4 + u // 8, u % 8 : u % 8 + 1, :] = recv_ref[pl.ds(place, 1), :]
            return 0

        lax.fori_loop(0, 8, take, 0)
        residual = rows_ref[...].reshape(256, PIVOTS) - prod_ref[top : top + 256, :]
        out_ref[top : top + 256, :] = dot3(residual, w_ref[...], NT)
        out = pltpu.make_async_copy(
            out_ref.at[pl.ds(top, 256)], out_hbm.at[pl.ds(top, 256)], osem.at[q]
        )
        out.start()
        outs.append(out)

    left(pair_v, 0)
    left(recv_ref.at[pl.ds(0, (DEVICES - 1) * CAP)], 8)
    left(rtgt_ref.at[pl.ds(0, DEVICES - 1)], 9)

    @pl.when(core == 0)
    def _():
        left(part, 2)
        left(all0.at[others], 4)
        left(all0, 6)

    @pl.when(core == 1)
    def _():
        left(pair_i, 1)
        left(all1.at[others], 2)
        left(all1.at[others], 4)
        left(all1, 6)

    for out in outs:
        out.wait()


def exchange(vectors, pivots, integrals, destination):
    vmem = pl.BlockSpec(memory_space=pltpu.VMEM)
    hbm = pl.BlockSpec(memory_space=pl.ANY)
    return pl.pallas_call(
        main_kernel,
        out_shape=jax.ShapeDtypeStruct((ROWS_DEV, PIVOTS), F32),
        in_specs=[pl.BlockSpec(memory_space=pltpu.SMEM), vmem, vmem, hbm, hbm],
        out_specs=hbm,
        scratch_shapes=[
            pltpu.VMEM((ROWS_DEV, PIVOTS), F32),
            pltpu.VMEM((ROWS_DEV + 8, VECS), F32),
            pltpu.VMEM((2, CHIPS, 2, 8, 128), F32),
            pltpu.VMEM((CHIPS, 8, 128), F32),
            pltpu.VMEM((CAP, DEVICES), I32),
            pltpu.SMEM((CAP, DEVICES), I32),
            pltpu.VMEM((DEVICES, CAP, PIVOTS), F32),
            pltpu.VMEM((DEVICES, 1, 128), I32),
            pltpu.VMEM((DEVICES, 1, 128), I32),
            pltpu.VMEM((CHIPS, 2, 8, 128), F32),
            pltpu.VMEM((CHIPS, 8, 128), F32),
            pltpu.VMEM((CHIPS, 3, 8, 128), F32),
            pltpu.VMEM((CHIPS - 1, 3, 8, 128), F32),
            pltpu.VMEM((3, 8, 128), F32),
            pltpu.VMEM((CHIPS, 3, 8, 128), F32),
            pltpu.VMEM((CHIPS, 2, 8, 128), F32),
            pltpu.VMEM((PIVOTS, PIVOTS), F32),
            pltpu.VMEM((PIVOTS, PIVOTS), F32),
            pltpu.VMEM((ROWS_DEV, PIVOTS), F32),
            pltpu.VMEM((DEVICES * CAP, PIVOTS), F32),
            pltpu.VMEM((32, 128), I32),
            pltpu.SMEM((32, 128), I32),
            pltpu.VMEM((32, 8, PIVOTS), F32),
            pltpu.VMEM((ROWS_DEV, PIVOTS), F32),
            pltpu.SemaphoreType.DMA((10,)),
            pltpu.SemaphoreType.DMA((10,)),
            pltpu.SemaphoreType.DMA((4,)),
            pltpu.SemaphoreType.DMA((4,)),
        ],
        compiler_params=pltpu.CompilerParams(collective_id=0, has_side_effects=True),
        name="exchange",
    )(pivots, pivots.reshape(1, -1), destination.reshape(1, -1), integrals, vectors)


def solution(mesh):
    return jax.shard_map(
        exchange,
        mesh=mesh,
        in_specs=(P(WIDE_NARROW, None), P(), P(WIDE_NARROW, None), P(WIDE_NARROW)),
        out_specs=P(WIDE_NARROW, None),
        check_vma=False,
    )
```

profile of v0, /device:TPU:1, one launch (start us, length us, event | category | flops | bytes accessed | tf_op | source)
XLA Modules:
  0.0 64.3 jit_solution(6021388626664636346)
XLA Ops:
  0.0 62.1 %exchange.1 = f32[1024,256]{1,0:T(8,128)} custom-call(s32[256]{0:T(256)} %piv_smem.1, s32[1,256]{1,0:T(1,128)} %bitcast.3, s32[1,1024]{1,0:T(1,128)} %bitcast.2, f32[1024,256]{1,0:T(8,128)} %ints_hbm.1, f32[1024,1024]{1,0:T(8,128)} %vec_hbm.1), custom_call_target="tpu_custom_call" | custom-call | tf_op jit(solution)/shard_map/exchange/pallas_call | solution.py:383
  62.1 2.3 %copy.6 = f32[1024,256]{1,0:T(8,128)} copy(f32[1024,256]{1,0:T(8,128)} %exchange.1) | data formatting | bytes 2097152
where the time goes:
time: 64.8 us; the launch traced here: 64.3 us
  Pallas kernels  62.1 us (96%)
  local copies, waits for them, and re-layouts  2.26 us (3%)
    pallas_call x1, Pallas kernels, exchange(): pl.pallas_call(main_kernel, out_shape=jax.ShapeDtypeStruct((ROWS_DEV, PIV...  62.1 us
    unnamed x1, local copies, waits for them, and re-layouts  2.26 us

commit v1 on v0

--- a/solution.py
+++ b/solution.py
@@ -160,7 +160,8 @@
     high = jnp.concatenate(highs, axis=1)
     place = dot_bf(high, jnp.concatenate(blocks, axis=1), NT) * CAP
     place = place + dot_bf(high, jnp.concatenate(slots, axis=1), NT)
-    return jnp.clip(place.astype(I32), 0, DEVICES * CAP - 1)
+    place = place.astype(I32)
+    return place // 8 * 16 + place % 8
 
 
 def far_first(offsets):
@@ -170,6 +171,7 @@
 
 
 CHIP_STEPS = far_first((z, x, y) for z in range(4) for x in range(4) for y in range(4) if (z, x, y) != (0, 0, 0))
+PLANE_ORDER = (2, 1, 3, 0)
 ALL_STEPS = far_first(
     (z, x, y, c)
     for z in range(4) for x in range(4) for y in range(4) for c in range(2)
@@ -178,10 +180,10 @@
 
 
 def main_kernel(
-    piv_smem, piv_ref, dest_ref, ints_hbm, vec_hbm, out_hbm,
+    piv_smem, piv_ref, dest_ref, ints_hbm, vec_hbm, out_ref,
     ints_ref, vec_ref, pvec_ref, pint_ref, from_ref, from_smem, send_ref, tgt_ref, rtgt_ref,
     pair_v, pair_i, mine, part, tile, all0, all1, a_ref, w_ref, prod_ref,
-    recv_ref, place_ref, place_smem, rows_ref, out_ref, ssem, rsem, lsem, osem,
+    recv_ref, place_ref, place_smem, rows_ref, ssem, rsem, lsem,
 ):
     wide, narrow = lax.axis_index("wide"), lax.axis_index("narrow")
     z, core, x, y = wide // 2, wide % 2, narrow // 4, narrow % 4
@@ -220,11 +222,13 @@
     pl.semaphore_wait(barrier, DEVICES - 1)
 
     sibling = at(0, 0, 0, 1)[0]
-    send(pvec_ref.at[1 - core], pair_v, 0, sibling)
-
-    @pl.when(core == 1)
-    def _():
-        send(pint_ref, pair_i, 1, sibling)
+    planes = [pl.ds(pl.multiple_of((z + dz) % 4 * 16, 16), 16) for dz in PLANE_ORDER]
+    for n, plane in enumerate(planes):
+        send(pvec_ref.at[1 - core, plane], pair_v.at[plane], 10 + n, sibling)
+
+        @pl.when(core == 1)
+        def _():
+            send(pint_ref.at[plane], pair_i.at[plane], 14 + n, sibling)
 
     source, target = slot_maps(dest)
     from_ref[...] = source
@@ -232,32 +236,35 @@
     to_smem = pltpu.make_async_copy(from_ref, from_smem, lsem.at[2])
     to_smem.start()
 
-    arrived(pair_v, 0)
-    mine[:, 0:2] = pvec_ref[core] + pair_v[...]
-
-    @pl.when(core == 0)
-    def _():
-        arrived(pair_i, 1)
-        mine[:, 2] = pint_ref[...] + pair_i[...]
-        for i, step in enumerate(CHIP_STEPS):
-            where, home = at(*step)
-            send(mine.at[home], part.at[i], 2, where)
-
     two = pl.ds(0, 2)
-
-    @pl.when(core == 1)
-    def _():
-        for i, step in enumerate(CHIP_STEPS):
-            where, home = at(*step)
-            send(mine.at[home, two], part.at[i, two], 2, where)
+    step_slot = {step: i for i, step in enumerate(CHIP_STEPS)}
+    for n, plane in enumerate(planes):
+        arrived(pair_v.at[plane], 10 + n)
+        mine[plane, 0:2] = pvec_ref[core, plane] + pair_v[plane]
+        group = [step for step in CHIP_STEPS if step[0] == PLANE_ORDER[n]]
+
+        @pl.when(core == 0)
+        def _():
+            arrived(pair_i.at[plane], 14 + n)
+            mine[plane, 2] = pint_ref[plane] + pair_i[plane]
+            for step in group:
+                where, home = at(*step)
+                send(mine.at[home], part.at[step_slot[step]], 2, where)
+
+        @pl.when(core == 1)
+        def _():
+            for step in group:
+                where, home = at(*step)
+                send(mine.at[home, two], part.at[step_slot[step], two], 2, where)
 
     to_smem.wait()
 
     def pack(d, _):
         for k in range(CAP):
-            send_ref[d, k : k + 1, :] = ints_ref[
-                pl.ds(jnp.clip(from_smem[k, d], 0, ROWS_DEV - 1), 1), :
-            ]
+            row = ints_ref[pl.ds(from_smem[k, d] & (ROWS_DEV - 1), 1), :]
+            send_ref[d, pl.ds(k // 8 * 16 + k % 8, 2, 8), :] = jnp.concatenate(
+                [row[:, :128], row[:, 128:]], axis=0
+            )
         return 0
 
     lax.fori_loop(0, DEVICES, pack, 0)
@@ -283,7 +290,7 @@
     for i, where in enumerate(steps):
         send(tgt_ref.at[where["wide"] * 16 + where["narrow"]], rtgt_ref.at[i], 9, where)
     rtgt_ref[DEVICES - 1] = tgt_ref[me]
-    recv_ref[(DEVICES - 1) * CAP :, :] = send_ref[me]
+    recv_ref[2 * (DEVICES - 1) * CAP :, :] = send_ref[me]
 
     @pl.when(core == 0)
     def _():
@@ -298,7 +305,7 @@
     for i, where in enumerate(steps):
         send(
             send_ref.at[where["wide"] * 16 + where["narrow"]],
-            recv_ref.at[pl.ds(i * CAP, CAP)], 8, where,
+            recv_ref.at[pl.ds(2 * i * CAP, 2 * CAP)], 8, where,
         )
 
     @pl.when(core == 0)
@@ -336,28 +343,23 @@
     place_copy = pltpu.make_async_copy(place_ref, place_smem, lsem.at[3])
     place_copy.start()
     place_copy.wait()
-    arrived(recv_ref.at[pl.ds(0, (DEVICES - 1) * CAP)], 8)
-    outs = []
+    arrived(recv_ref.at[pl.ds(0, 2 * (DEVICES - 1) * CAP)], 8)
     for q in range(4):
         top = q * 256
 
         def take(t, _, q=q):
             for u in range(32):
-                place = jnp.clip(place_smem[q * 8 + t, u], 0, DEVICES * CAP - 1)
-                rows_ref[t * 4 + u // 8, u % 8 : u % 8 + 1, :] = recv_ref[pl.ds(place, 1), :]
+                line = place_smem[q * 8 + t, u] & (2 * DEVICES * CAP - 9)
+                rows_ref[t * 4 + u // 8, pl.ds(u % 8, 2, 8), :] = recv_ref[pl.ds(line, 2, 8), :]
             return 0
 
         lax.fori_loop(0, 8, take, 0)
-        residual = rows_ref[...].reshape(256, PIVOTS) - prod_ref[top : top + 256, :]
-        out_ref[top : top + 256, :] = dot3(residual, w_ref[...], NT)
-        out = pltpu.make_async_copy(
-            out_ref.at[pl.ds(top, 256)], out_hbm.at[pl.ds(top, 256)], osem.at[q]
-        )
-        out.start()
-        outs.append(out)
-
-    left(pair_v, 0)
-    left(recv_ref.at[pl.ds(0, (DEVICES - 1) * CAP)], 8)
+        rows = jnp.concatenate([rows_ref[:, h * 8 : h * 8 + 8].reshape(256, 128) for h in range(2)], axis=1)
+        out_ref[top : top + 256, :] = dot3(rows - prod_ref[top : top + 256, :], w_ref[...], NT)
+
+    for n, plane in enumerate(planes):
+        left(pair_v.at[plane], 10 + n)
+    left(recv_ref.at[pl.ds(0, 2 * (DEVICES - 1) * CAP)], 8)
     left(rtgt_ref.at[pl.ds(0, DEVICES - 1)], 9)
 
     @pl.when(core == 0)
@@ -368,23 +370,24 @@
 
     @pl.when(core == 1)
     def _():
-        left(pair_i, 1)
+        for n, plane in enumerate(planes):
+            left(pair_i.at[plane], 14 + n)
         left(all1.at[others], 2)
         left(all1.at[others], 4)
         left(all1, 6)
 
-    for out in outs:
-        out.wait()
+
+VMEM_LIMIT = 52 << 20
 
 
 def exchange(vectors, pivots, integrals, destination):
     vmem = pl.BlockSpec(memory_space=pltpu.VMEM)
-    hbm = pl.BlockSpec(memory_space=pl.ANY)
+    hbm = pl.BlockSpec(memory_space=pltpu.HBM)
     return pl.pallas_call(
         main_kernel,
         out_shape=jax.ShapeDtypeStruct((ROWS_DEV, PIVOTS), F32),
         in_specs=[pl.BlockSpec(memory_space=pltpu.SMEM), vmem, vmem, hbm, hbm],
-        out_specs=hbm,
+        out_specs=vmem,
         scratch_shapes=[
             pltpu.VMEM((ROWS_DEV, PIVOTS), F32),
             pltpu.VMEM((ROWS_DEV + 8, VECS), F32),
@@ -392,7 +395,7 @@
             pltpu.VMEM((CHIPS, 8, 128), F32),
             pltpu.VMEM((CAP, DEVICES), I32),
             pltpu.SMEM((CAP, DEVICES), I32),
-            pltpu.VMEM((DEVICES, CAP, PIVOTS), F32),
+            pltpu.VMEM((DEVICES, 2 * CAP, 128), F32),
             pltpu.VMEM((DEVICES, 1, 128), I32),
             pltpu.VMEM((DEVICES, 1, 128), I32),
             pltpu.VMEM((CHIPS, 2, 8, 128), F32),
@@ -405,17 +408,17 @@
             pltpu.VMEM((PIVOTS, PIVOTS), F32),
             pltpu.VMEM((PIVOTS, PIVOTS), F32),
             pltpu.VMEM((ROWS_DEV, PIVOTS), F32),
-            pltpu.VMEM((DEVICES * CAP, PIVOTS), F32),
+            pltpu.VMEM((2 * DEVICES * CAP, 128), F32),
             pltpu.VMEM((32, 128), I32),
             pltpu.SMEM((32, 128), I32),
-            pltpu.VMEM((32, 8, PIVOTS), F32),
-            pltpu.VMEM((ROWS_DEV, PIVOTS), F32),
-            pltpu.SemaphoreType.DMA((10,)),
-            pltpu.SemaphoreType.DMA((10,)),
-            pltpu.SemaphoreType.DMA((4,)),
+            pltpu.VMEM((32, 16, 128), F32),
+            pltpu.SemaphoreType.DMA((18,)),
+            pltpu.SemaphoreType.DMA((18,)),
             pltpu.SemaphoreType.DMA((4,)),
         ],
-        compiler_params=pltpu.CompilerParams(collective_id=0, has_side_effects=True),
+        compiler_params=pltpu.CompilerParams(
+            collective_id=0, has_side_effects=True, vmem_limit_bytes=VMEM_LIMIT
+        ),
         name="exchange",
     )(pivots, pivots.reshape(1, -1), destination.reshape(1, -1), integrals, vectors)
 

time: 64.8 us -> 61.9 us (0.955)
  Pallas kernels: 62.1 us -> 59.4 us
    pallas_call x1, Pallas kernels: 62.1 us -> 59.4 us  [exchange(): pl.pallas_call(main_kernel, out_shape=jax.ShapeDtypeStruct((ROWS_DEV, PIV...]
    unnamed x1 -> x5, local copies, waits for them, and re-layouts: 2.26 us -> 2.34 us
where the time goes in v1:
time: 61.9 us; the launch traced here: 61.8 us
  Pallas kernels  59.4 us (96%)
  local copies, waits for them, and re-layouts  2.34 us (4%)
    pallas_call x1, Pallas kernels, exchange(): pl.pallas_call(main_kernel, out_shape=jax.ShapeDtypeStruct((ROWS_DEV, PIV...  59.4 us
    unnamed x5, local copies, waits for them, and re-layouts  2.34 us

profile of v1, /device:TPU:1, one launch (start us, length us, event | category | flops | bytes accessed | tf_op | source)
XLA Modules:
  0.0 61.8 jit_solution(14369432321164233325)
XLA Ops:
  0.0 0.0 copy-start
  0.0 0.7 %copy-done = s32[1024]{0:T(1024)S(1)} copy-done((s32[1024]{0:T(1024)S(1)}, s32[1024]{0:T(1024)}, u32[]{:S(2)}) %copy-start) | copy-done | bytes 4120
  0.7 0.0 copy-start.1
  0.7 0.7 %copy-done.1 = s32[256]{0:T(256)S(1)} copy-done((s32[256]{0:T(256)S(1)}, s32[256]{0:T(256)}, u32[]{:S(2)}) %copy-start.1) | copy-done | bytes 1048
  1.4 59.4 %exchange.1 = f32[1024,256]{1,0:T(8,128)S(1)} custom-call(s32[256]{0:T(256)S(1)} %copy-done.1, s32[1,256]{1,0:T(1,128)S(1)} %bitcast.3, s32[1,1024]{1,0:T(1,128)S(1)} %bitcast.2, f32[1024,256]{1,0:T(8,128)} %ints_hbm.1, f32[1024,1024]{1,0:T(8,128)} %vec_hbm.1), custom_call_target="tpu_custom_call" | custom-call | tf_op jit(solution)/shard_map/exchange/pallas_call | solution.py:386
  60.8 1.0 %copy.6 = f32[1024,256]{1,0:T(8,128)} copy(f32[1024,256]{1,0:T(8,128)S(1)} %exchange.1) | data formatting | bytes 2097152
Async XLA Ops:
  0.0 0.7 %copy-start = (s32[1024]{0:T(1024)S(1)}, s32[1024]{0:T(1024)}, u32[]{:S(2)}) copy-start(s32[1024]{0:T(1024)} %param.7) | copy-start | bytes 12292
  0.7 0.7 %copy-start.1 = (s32[256]{0:T(256)S(1)}, s32[256]{0:T(256)}, u32[]{:S(2)}) copy-start(s32[256]{0:T(256)} %piv_smem.1) | copy-start | bytes 3076

commit v2 on v1

--- a/solution.py
+++ b/solution.py
@@ -32,23 +32,32 @@
     inside = (lanes >= at) & (lanes < at + BLOCK)
     t = jnp.where(inside, s, (rows == lanes - other).astype(F32))
     done = []
+    c0 = jnp.broadcast_to(t[:, at : at + 1], t.shape)
+    c1 = jnp.broadcast_to(t[:, at + 1 : at + 2], t.shape)
     for j in range(0, BLOCK, 2):
-        top = j // 8 * 8
-        i = j - top
+        i = j % 8
         r0, r1 = t[i : i + 1, :], t[i + 1 : i + 2, :]
-        c0 = jnp.broadcast_to(t[:, at + j : at + j + 1], t.shape)
-        c1 = jnp.broadcast_to(t[:, at + j + 1 : at + j + 2], t.shape)
         a, b, c = c0[i : i + 1, :], c0[i + 1 : i + 2, :], c1[i + 1 : i + 2, :]
         inv = 1.0 / (a * c - b * b)
-        u0 = (c * inv) * r0 - (b * inv) * r1
-        u1 = (a * inv) * r1 - (b * inv) * r0
+        p, q, s = c * inv, b * inv, a * inv
         ia = 1.0 / a
         done.append(r0 * lax.rsqrt(a))
         done.append((r1 - (b * ia) * r0) * lax.rsqrt(c - b * (b * ia)))
+        if j + 2 == BLOCK:
+            break
+        old = t
+        u0 = p * r0 - q * r1
+        u1 = s * r1 - q * r0
         below = lax.broadcasted_iota(I32, t.shape, 0) > i + 1
         t = jnp.where(below, t - c0 * u0 - c1 * u1, t)
+        nexts = []
+        for k in (2, 3):
+            x0, x1 = c0[i + k : i + k + 1, :], c1[i + k : i + k + 1, :]
+            col = jnp.broadcast_to(old[:, at + j + k : at + j + k + 1], t.shape)
+            nexts.append(col - c0 * (p * x0 - q * x1) - c1 * (s * x1 - q * x0))
+        c0, c1 = nexts
         if (j + 2) % 8 == 0:
-            t = t[8:, :]
+            t, c0, c1 = t[8:, :], c0[8:, :], c1[8:, :]
     full = jnp.concatenate(done, axis=0)
     return full[:, other : other + BLOCK]
 
@@ -85,11 +94,14 @@
     return hi, mid, (rest - mid.astype(F32)).astype(BF16)
 
 
+def split2(x):
+    hi = x.astype(BF16)
+    return hi, (x - hi.astype(F32)).astype(BF16)
+
+
 def dot3(a, b, dims):
-    ah = a.astype(BF16)
-    al = (a - ah.astype(F32)).astype(BF16)
-    bh = b.astype(BF16)
-    bl = (b - bh.astype(F32)).astype(BF16)
+    ah, al = split2(a)
+    bh, bl = split2(b)
     return dot_bf(ah, bh, dims) + (dot_bf(ah, bl, dims) + dot_bf(al, bh, dims))
 
 
@@ -110,7 +122,7 @@
 def own_pivot_vectors(piv_smem, first, vec_ref, pvec_ref):
     def pick(t, _):
         for u in range(8):
-            row = piv_smem[t * 8 + u] - first
+            row = piv_smem[0, t * 8 + u] - first
             mine = (row >= 0) & (row < ROWS_DEV)
             values = vec_ref[pl.ds(jnp.where(mine, row, ROWS_DEV), 1), :]
             for ct in range(VECS // 128):
@@ -172,6 +184,7 @@
 
 CHIP_STEPS = far_first((z, x, y) for z in range(4) for x in range(4) for y in range(4) if (z, x, y) != (0, 0, 0))
 PLANE_ORDER = (2, 1, 3, 0)
+ROW_SPLIT = (0, 0)
 ALL_STEPS = far_first(
     (z, x, y, c)
     for z in range(4) for x in range(4) for y in range(4) for c in range(2)
@@ -180,10 +193,10 @@
 
 
 def main_kernel(
-    piv_smem, piv_ref, dest_ref, ints_hbm, vec_hbm, out_ref,
-    ints_ref, vec_ref, pvec_ref, pint_ref, from_ref, from_smem, send_ref, tgt_ref, rtgt_ref,
+    index_ref, ints_hbm, vec_hbm, out_ref,
+    piv_smem, ints_ref, vec_ref, pvec_ref, pint_ref, from_ref, from_smem, send_ref, tgt_ref, rtgt_ref,
     pair_v, pair_i, mine, part, tile, all0, all1, a_ref, w_ref, prod_ref,
-    recv_ref, place_ref, place_smem, rows_ref, ssem, rsem, lsem,
+    recv_ref, place_ref, place_smem, rows_ref, vh_ref, vl_ref, ssem, rsem, lsem,
 ):
     wide, narrow = lax.axis_index("wide"), lax.axis_index("narrow")
     z, core, x, y = wide // 2, wide % 2, narrow // 4, narrow % 4
@@ -210,14 +223,17 @@
     load_vec.start()
     load_ints = pltpu.make_async_copy(ints_hbm, ints_ref, lsem.at[1])
     load_ints.start()
+    load_piv = pltpu.make_async_copy(index_ref.at[:, pl.ds(0, PIVOTS)], piv_smem, lsem.at[3])
+    load_piv.start()
     barrier = pltpu.get_barrier_semaphore()
     for step in ALL_STEPS:
         pl.semaphore_signal(barrier, inc=1, device_id=at(*step)[0], device_id_type=pl.DeviceIdType.MESH)
     vec_ref[pl.ds(ROWS_DEV, 8), :] = jnp.zeros((8, VECS), F32)
-    dest = dest_ref[...]
+    dest = index_ref[:, PIVOTS:]
     load_ints.wait()
-    own_pivot_integrals(piv_ref[...], dest, ints_ref, pint_ref)
+    own_pivot_integrals(index_ref[:, :PIVOTS], dest, ints_ref, pint_ref)
     load_vec.wait()
+    load_piv.wait()
     own_pivot_vectors(piv_smem, me * ROWS_DEV, vec_ref, pvec_ref)
     pl.semaphore_wait(barrier, DEVICES - 1)
 
@@ -268,6 +284,16 @@
         return 0
 
     lax.fori_loop(0, DEVICES, pack, 0)
+    steps = [at(*step)[0] for step in ALL_STEPS]
+
+    def rows_out(begin, end):
+        for i in range(begin, end):
+            send(
+                send_ref.at[steps[i]["wide"] * 16 + steps[i]["narrow"]],
+                recv_ref.at[pl.ds(2 * i * CAP, 2 * CAP)], 8, steps[i],
+            )
+
+    rows_out(0, ROW_SPLIT[0])
     others = pl.ds(0, CHIPS - 1)
 
     @pl.when(core == 0)
@@ -286,10 +312,17 @@
             send(tile.at[two], all1.at[chip], 4, at(*step)[0])
         all1[chip] = tile[0:2]
 
-    steps = [at(*step)[0] for step in ALL_STEPS]
     for i, where in enumerate(steps):
         send(tgt_ref.at[where["wide"] * 16 + where["narrow"]], rtgt_ref.at[i], 9, where)
     rtgt_ref[DEVICES - 1] = tgt_ref[me]
+    rows_out(ROW_SPLIT[0], ROW_SPLIT[1])
+
+    def halve(t, _):
+        span = pl.ds(pl.multiple_of(t * 64, 64), 64)
+        vh_ref[span, :], vl_ref[span, :] = split2(vec_ref[span, :])
+        return 0
+
+    lax.fori_loop(0, ROWS_DEV // 64, halve, 0)
     recv_ref[2 * (DEVICES - 1) * CAP :, :] = send_ref[me]
 
     @pl.when(core == 0)
@@ -302,11 +335,7 @@
         arrived(all1.at[others], 4)
         send(all1, all1, 6, sibling)
 
-    for i, where in enumerate(steps):
-        send(
-            send_ref.at[where["wide"] * 16 + where["narrow"]],
-            recv_ref.at[pl.ds(2 * i * CAP, 2 * CAP)], 8, where,
-        )
+    rows_out(ROW_SPLIT[1], DEVICES - 1)
 
     @pl.when(core == 0)
     def _():
@@ -334,10 +363,13 @@
         block = block - dot_hi(cols, cols, NT)
     a_ref[...] = (block + block.T) * 0.5
     invert_factor(a_ref, w_ref)
-    prod_ref[...] = sum(
-        dot3(vec_ref[:ROWS_DEV, ct * 256 : ct * 256 + 256], pivot_columns(ct), NT)
-        for ct in range(VECS // 256)
-    )
+    product = jnp.zeros((ROWS_DEV, PIVOTS), F32)
+    for ct in range(VECS // 256):
+        span = slice(ct * 256, ct * 256 + 256)
+        ph, pl_ = split2(pivot_columns(ct))
+        vh = vh_ref[:, span]
+        product = product + (dot_bf(vh, ph, NT) + (dot_bf(vh, pl_, NT) + dot_bf(vl_ref[:, span], ph, NT)))
+    prod_ref[...] = product
     arrived(rtgt_ref.at[pl.ds(0, DEVICES - 1)], 9)
     place_ref[...] = row_places(rtgt_ref[...].reshape(DEVICES, 128))
     place_copy = pltpu.make_async_copy(place_ref, place_smem, lsem.at[3])
@@ -386,9 +418,10 @@
     return pl.pallas_call(
         main_kernel,
         out_shape=jax.ShapeDtypeStruct((ROWS_DEV, PIVOTS), F32),
-        in_specs=[pl.BlockSpec(memory_space=pltpu.SMEM), vmem, vmem, hbm, hbm],
+        in_specs=[vmem, hbm, hbm],
         out_specs=vmem,
         scratch_shapes=[
+            pltpu.SMEM((1, PIVOTS), I32),
             pltpu.VMEM((ROWS_DEV, PIVOTS), F32),
             pltpu.VMEM((ROWS_DEV + 8, VECS), F32),
             pltpu.VMEM((2, CHIPS, 2, 8, 128), F32),
@@ -412,6 +445,8 @@
             pltpu.VMEM((32, 128), I32),
             pltpu.SMEM((32, 128), I32),
             pltpu.VMEM((32, 16, 128), F32),
+            pltpu.VMEM((ROWS_DEV, VECS), BF16),
+            pltpu.VMEM((ROWS_DEV, VECS), BF16),
             pltpu.SemaphoreType.DMA((18,)),
             pltpu.SemaphoreType.DMA((18,)),
             pltpu.SemaphoreType.DMA((4,)),
@@ -420,7 +455,7 @@
             collective_id=0, has_side_effects=True, vmem_limit_bytes=VMEM_LIMIT
         ),
         name="exchange",
-    )(pivots, pivots.reshape(1, -1), destination.reshape(1, -1), integrals, vectors)
+    )(jnp.concatenate([pivots, destination]).reshape(1, -1), integrals, vectors)
 
 
 def solution(mesh):

time: 61.9 us -> 60.8 us (0.982)
  local copies, waits for them, and re-layouts: 2.34 us -> 0.98 us
  other arithmetic: 0 us -> 0.7 us
    unnamed x5 -> x1, local copies, waits for them, and re-layouts: 2.34 us -> 0.97 us
    concatenate x0 -> x1, other arithmetic: none -> 0.7 us  [exchange(): jnp.concatenate([pivots, destination]).reshape(1, -1)]
where the time goes in v2:
time: 60.8 us; the launch traced here: 60.6 us
  Pallas kernels  58.9 us (97%)
  local copies, waits for them, and re-layouts  0.98 us (2%)
  other arithmetic  0.7 us (1%)
    pallas_call x1, Pallas kernels, exchange(): pl.pallas_call(main_kernel, out_shape=jax.ShapeDtypeStruct((ROWS_DEV, PIV...  58.9 us

profile of v2, /device:TPU:1, one launch (start us, length us, event | category | flops | bytes accessed | tf_op | source)
XLA Modules:
  0.0 60.6 jit_solution(2650902592855874448)
XLA Ops:
  0.0 0.7 %pad_add_fusion = s32[1280]{0:T(1024)S(1)} fusion(s32[1024]{0:T(1024)} %param.7, s32[256]{0:T(256)} %param.5), kind=kLoop, calls=%fused_computation | loop fusion | flops 1280 | bytes 10240 | tf_op jit(solution)/shard_map/concatenate | solution.py:458
  0.7 58.9 %exchange.1 = f32[1024,256]{1,0:T(8,128)S(1)} custom-call(s32[1,1280]{1,0:T(1,128)S(1)} %reshape.3.index_ref, f32[1024,256]{1,0:T(8,128)} %ints_hbm.1, f32[1024,1024]{1,0:T(8,128)} %vec_hbm.1), custom_call_target="tpu_custom_call" | custom-call | tf_op jit(solution)/shard_map/exchange/pallas_call | solution.py:418
  59.7 1.0 %copy.6 = f32[1024,256]{1,0:T(8,128)} copy(f32[1024,256]{1,0:T(8,128)S(1)} %exchange.1) | data formatting | bytes 2097152
  (1 shorter events, 0.0 us)

commit v3 on v2

--- a/solution.py
+++ b/solution.py
@@ -99,12 +99,6 @@
     return hi, (x - hi.astype(F32)).astype(BF16)
 
 
-def dot3(a, b, dims):
-    ah, al = split2(a)
-    bh, bl = split2(b)
-    return dot_bf(ah, bh, dims) + (dot_bf(ah, bl, dims) + dot_bf(al, bh, dims))
-
-
 def column(row):
     return jnp.broadcast_to(row.astype(F32), (128, row.shape[1])).T.astype(I32)
 
@@ -196,7 +190,7 @@
     index_ref, ints_hbm, vec_hbm, out_ref,
     piv_smem, ints_ref, vec_ref, pvec_ref, pint_ref, from_ref, from_smem, send_ref, tgt_ref, rtgt_ref,
     pair_v, pair_i, mine, part, tile, all0, all1, a_ref, w_ref, prod_ref,
-    recv_ref, place_ref, place_smem, rows_ref, vh_ref, vl_ref, ssem, rsem, lsem,
+    recv_ref, place_ref, place_smem, rows_ref, vh_ref, vl_ref, wh_ref, wl_ref, ssem, rsem, lsem,
 ):
     wide, narrow = lax.axis_index("wide"), lax.axis_index("narrow")
     z, core, x, y = wide // 2, wide % 2, narrow // 4, narrow % 4
@@ -363,6 +357,7 @@
         block = block - dot_hi(cols, cols, NT)
     a_ref[...] = (block + block.T) * 0.5
     invert_factor(a_ref, w_ref)
+    wh_ref[...], wl_ref[...] = split2(w_ref[...])
     product = jnp.zeros((ROWS_DEV, PIVOTS), F32)
     for ct in range(VECS // 256):
         span = slice(ct * 256, ct * 256 + 256)
@@ -376,18 +371,31 @@
     place_copy.start()
     place_copy.wait()
     arrived(recv_ref.at[pl.ds(0, 2 * (DEVICES - 1) * CAP)], 8)
-    for q in range(4):
-        top = q * 256
-
-        def take(t, _, q=q):
+
+    def take(q):
+        for t in range(CHUNK // 32):
             for u in range(32):
-                line = place_smem[q * 8 + t, u] & (2 * DEVICES * CAP - 9)
+                line = place_smem[q * (CHUNK // 32) + t, u] & (2 * DEVICES * CAP - 9)
                 rows_ref[t * 4 + u // 8, pl.ds(u % 8, 2, 8), :] = recv_ref[pl.ds(line, 2, 8), :]
-            return 0
-
-        lax.fori_loop(0, 8, take, 0)
-        rows = jnp.concatenate([rows_ref[:, h * 8 : h * 8 + 8].reshape(256, 128) for h in range(2)], axis=1)
-        out_ref[top : top + 256, :] = dot3(rows - prod_ref[top : top + 256, :], w_ref[...], NT)
+
+    def finish(q, rows):
+        span = pl.ds(pl.multiple_of(q * CHUNK, CHUNK), CHUNK)
+        rh, rl = split2(rows - prod_ref[span, :])
+        wh = wh_ref[...]
+        out_ref[span, :] = dot_bf(rh, wh, NT) + (dot_bf(rh, wl_ref[...], NT) + dot_bf(rl, wh, NT))
+
+    def gathered():
+        return jnp.concatenate([rows_ref[:, h * 8 : h * 8 + 8].reshape(CHUNK, 128) for h in range(2)], axis=1)
+
+    def step(q, _):
+        rows = gathered()
+        take(q + 1)
+        finish(q, rows)
+        return 0
+
+    take(0)
+    lax.fori_loop(0, ROWS_DEV // CHUNK - 1, step, 0)
+    finish(ROWS_DEV // CHUNK - 1, gathered())
 
     for n, plane in enumerate(planes):
         left(pair_v.at[plane], 10 + n)
@@ -410,6 +418,7 @@
 
 
 VMEM_LIMIT = 52 << 20
+CHUNK = 128
 
 
 def exchange(vectors, pivots, integrals, destination):
@@ -444,9 +453,11 @@
             pltpu.VMEM((2 * DEVICES * CAP, 128), F32),
             pltpu.VMEM((32, 128), I32),
             pltpu.SMEM((32, 128), I32),
-            pltpu.VMEM((32, 16, 128), F32),
+            pltpu.VMEM((CHUNK // 8, 16, 128), F32),
             pltpu.VMEM((ROWS_DEV, VECS), BF16),
             pltpu.VMEM((ROWS_DEV, VECS), BF16),
+            pltpu.VMEM((PIVOTS, PIVOTS), BF16),
+            pltpu.VMEM((PIVOTS, PIVOTS), BF16),
             pltpu.SemaphoreType.DMA((18,)),
             pltpu.SemaphoreType.DMA((18,)),
             pltpu.SemaphoreType.DMA((4,)),

time: 60.8 us -> 60.3 us (level)
  no operation moved by 1% of the time
where the time goes in v3:
time: 60.3 us; the launch traced here: 60.2 us
  Pallas kernels  58.5 us (97%)
  local copies, waits for them, and re-layouts  0.98 us (2%)
  other arithmetic  0.7 us (1%)
    pallas_call x1, Pallas kernels, exchange(): pl.pallas_call(main_kernel, out_shape=jax.ShapeDtypeStruct((ROWS_DEV, PIV...  58.5 us

profile of v3, /device:TPU:1, one launch (start us, length us, event | category | flops | bytes accessed | tf_op | source)
XLA Modules:
  0.0 60.2 jit_solution(5493230925765939094)
XLA Ops:
  0.0 0.7 %pad_add_fusion = s32[1280]{0:T(1024)S(1)} fusion(s32[1024]{0:T(1024)} %param.7, s32[256]{0:T(256)} %param.5), kind=kLoop, calls=%fused_computation | loop fusion | flops 1280 | bytes 10240 | tf_op jit(solution)/shard_map/concatenate | solution.py:469
  0.7 58.5 %exchange.1 = f32[1024,256]{1,0:T(8,128)S(1)} custom-call(s32[1,1280]{1,0:T(1,128)S(1)} %reshape.3.index_ref, f32[1024,256]{1,0:T(8,128)} %ints_hbm.1, f32[1024,1024]{1,0:T(8,128)} %vec_hbm.1), custom_call_target="tpu_custom_call" | custom-call | tf_op jit(solution)/shard_map/exchange/pallas_call | solution.py:427
  59.2 1.0 %copy.6 = f32[1024,256]{1,0:T(8,128)} copy(f32[1024,256]{1,0:T(8,128)S(1)} %exchange.1) | data formatting | bytes 2097152
  (1 shorter events, 0.0 us)

commit v4 on v3

--- a/solution.py
+++ b/solution.py
@@ -172,7 +172,7 @@
 
 def far_first(offsets):
     offsets = list(offsets)
-    random.Random(7).shuffle(offsets)
+    random.Random(3).shuffle(offsets)
     return sorted(offsets, key=lambda o: -sum(min(v, 4 - v) for v in o[:3]))
 
 
@@ -418,7 +418,7 @@
 
 
 VMEM_LIMIT = 52 << 20
-CHUNK = 128
+CHUNK = 256
 
 
 def exchange(vectors, pivots, integrals, destination):

time: 60.3 us -> 59.3 us (0.983)
  Pallas kernels: 58.5 us -> 57.4 us
    pallas_call x1, Pallas kernels: 58.5 us -> 57.4 us  [exchange(): pl.pallas_call(main_kernel, out_shape=jax.ShapeDtypeStruct((ROWS_DEV, PIV...]
where the time goes in v4:
time: 59.3 us; the launch traced here: 59.1 us
  Pallas kernels  57.4 us (97%)
  local copies, waits for them, and re-layouts  0.98 us (2%)
  other arithmetic  0.7 us (1%)
    pallas_call x1, Pallas kernels, exchange(): pl.pallas_call(main_kernel, out_shape=jax.ShapeDtypeStruct((ROWS_DEV, PIV...  57.4 us

profile of v4, /device:TPU:1, one launch (start us, length us, event | category | flops | bytes accessed | tf_op | source)
XLA Modules:
  0.0 59.1 jit_solution(13035587260477754493)
XLA Ops:
  0.0 0.7 %pad_add_fusion = s32[1280]{0:T(1024)S(1)} fusion(s32[1024]{0:T(1024)} %param.7, s32[256]{0:T(256)} %param.5), kind=kLoop, calls=%fused_computation | loop fusion | flops 1280 | bytes 10240 | tf_op jit(solution)/shard_map/concatenate | solution.py:469
  0.7 57.4 %exchange.1 = f32[1024,256]{1,0:T(8,128)S(1)} custom-call(s32[1,1280]{1,0:T(1,128)S(1)} %reshape.3.index_ref, f32[1024,256]{1,0:T(8,128)} %ints_hbm.1, f32[1024,1024]{1,0:T(8,128)} %vec_hbm.1), custom_call_target="tpu_custom_call" | custom-call | tf_op jit(solution)/shard_map/exchange/pallas_call | solution.py:427
  58.2 1.0 %copy.6 = f32[1024,256]{1,0:T(8,128)} copy(f32[1024,256]{1,0:T(8,128)S(1)} %exchange.1) | data formatting | bytes 2097152
  (1 shorter events, 0.0 us)

commit v5 on v4

--- a/solution.py
+++ b/solution.py
@@ -108,7 +108,7 @@
     match = bf(
         jnp.concatenate([piv_col == dest[:, i : i + 128] for i in range(0, ROWS_DEV, 128)], axis=1)
     )
-    rows = sum(dot_bf(match, part) for part in split3(ints_ref[...]))
+    rows = sum(dot_bf(match, part) for part in split3(ints_ref[:ROWS_DEV, :]))
     for ct in range(PIVOTS // 128):
         pint_ref[ct * 32 : ct * 32 + 32] = rows[:, ct * 128 : ct * 128 + 128].reshape(32, 8, 128)
 
@@ -215,7 +215,7 @@
 
     load_vec = pltpu.make_async_copy(vec_hbm, vec_ref.at[pl.ds(0, ROWS_DEV)], lsem.at[0])
     load_vec.start()
-    load_ints = pltpu.make_async_copy(ints_hbm, ints_ref, lsem.at[1])
+    load_ints = pltpu.make_async_copy(ints_hbm, ints_ref.at[pl.ds(0, ROWS_DEV)], lsem.at[1])
     load_ints.start()
     load_piv = pltpu.make_async_copy(index_ref.at[:, pl.ds(0, PIVOTS)], piv_smem, lsem.at[3])
     load_piv.start()
@@ -317,7 +317,7 @@
         return 0
 
     lax.fori_loop(0, ROWS_DEV // 64, halve, 0)
-    recv_ref[2 * (DEVICES - 1) * CAP :, :] = send_ref[me]
+    recv_ref[2 * (DEVICES - 1) * CAP : 2 * DEVICES * CAP, :] = send_ref[me]
 
     @pl.when(core == 0)
     def _():
@@ -385,7 +385,7 @@
         out_ref[span, :] = dot_bf(rh, wh, NT) + (dot_bf(rh, wl_ref[...], NT) + dot_bf(rl, wh, NT))
 
     def gathered():
-        return jnp.concatenate([rows_ref[:, h * 8 : h * 8 + 8].reshape(CHUNK, 128) for h in range(2)], axis=1)
+        return jnp.concatenate([rows_ref[: CHUNK // 8, h * 8 : h * 8 + 8].reshape(CHUNK, 128) for h in range(2)], axis=1)
 
     def step(q, _):
         rows = gathered()
@@ -431,13 +431,13 @@
         out_specs=vmem,
         scratch_shapes=[
             pltpu.SMEM((1, PIVOTS), I32),
-            pltpu.VMEM((ROWS_DEV, PIVOTS), F32),
+            pltpu.VMEM((ROWS_DEV + 32, PIVOTS), F32),
             pltpu.VMEM((ROWS_DEV + 8, VECS), F32),
-            pltpu.VMEM((2, CHIPS, 2, 8, 128), F32),
+            pltpu.VMEM((3, CHIPS, 2, 8, 128), F32),
             pltpu.VMEM((CHIPS, 8, 128), F32),
             pltpu.VMEM((CAP, DEVICES), I32),
             pltpu.SMEM((CAP, DEVICES), I32),
-            pltpu.VMEM((DEVICES, 2 * CAP, 128), F32),
+            pltpu.VMEM((DEVICES + 2, 2 * CAP, 128), F32),
             pltpu.VMEM((DEVICES, 1, 128), I32),
             pltpu.VMEM((DEVICES, 1, 128), I32),
             pltpu.VMEM((CHIPS, 2, 8, 128), F32),
@@ -450,10 +450,10 @@
             pltpu.VMEM((PIVOTS, PIVOTS), F32),
             pltpu.VMEM((PIVOTS, PIVOTS), F32),
             pltpu.VMEM((ROWS_DEV, PIVOTS), F32),
-            pltpu.VMEM((2 * DEVICES * CAP, 128), F32),
+            pltpu.VMEM((2 * DEVICES * CAP + 64, 128), F32),
             pltpu.VMEM((32, 128), I32),
             pltpu.SMEM((32, 128), I32),
-            pltpu.VMEM((CHUNK // 8, 16, 128), F32),
+            pltpu.VMEM((CHUNK // 8 + 4, 16, 128), F32),
             pltpu.VMEM((ROWS_DEV, VECS), BF16),
             pltpu.VMEM((ROWS_DEV, VECS), BF16),
             pltpu.VMEM((PIVOTS, PIVOTS), BF16),

time: 59.3 us -> 59.3 us (level)
  no operation moved by 1% of the time
where the time goes in v5:
time: 59.3 us; the launch traced here: 59.1 us
  Pallas kernels  57.4 us (97%)
  local copies, waits for them, and re-layouts  0.98 us (2%)
  other arithmetic  0.7 us (1%)
    pallas_call x1, Pallas kernels, exchange(): pl.pallas_call(main_kernel, out_shape=jax.ShapeDtypeStruct((ROWS_DEV, PIV...  57.4 us

profile of v5, /device:TPU:1, one launch (start us, length us, event | category | flops | bytes accessed | tf_op | source)
XLA Modules:
  0.0 59.1 jit_solution(2230259012628358124)
XLA Ops:
  0.0 0.7 %pad_add_fusion = s32[1280]{0:T(1024)S(1)} fusion(s32[1024]{0:T(1024)} %param.7, s32[256]{0:T(256)} %param.5), kind=kLoop, calls=%fused_computation | loop fusion | flops 1280 | bytes 10240 | tf_op jit(solution)/shard_map/concatenate | solution.py:469
  0.7 57.4 %exchange.1 = f32[1024,256]{1,0:T(8,128)S(1)} custom-call(s32[1,1280]{1,0:T(1,128)S(1)} %reshape.3.index_ref, f32[1024,256]{1,0:T(8,128)} %ints_hbm.1, f32[1024,1024]{1,0:T(8,128)} %vec_hbm.1), custom_call_target="tpu_custom_call" | custom-call | tf_op jit(solution)/shard_map/exchange/pallas_call | solution.py:427
  58.2 1.0 %copy.6 = f32[1024,256]{1,0:T(8,128)} copy(f32[1024,256]{1,0:T(8,128)S(1)} %exchange.1) | data formatting | bytes 2097152
  (1 shorter events, 0.0 us)

commit v6 on v5

--- a/solution.py
+++ b/solution.py
@@ -166,7 +166,7 @@
     high = jnp.concatenate(highs, axis=1)
     place = dot_bf(high, jnp.concatenate(blocks, axis=1), NT) * CAP
     place = place + dot_bf(high, jnp.concatenate(slots, axis=1), NT)
-    place = place.astype(I32)
+    place = jnp.clip(place.astype(I32), 0, DEVICES * CAP - 1)
     return place // 8 * 16 + place % 8
 
 
@@ -375,7 +375,7 @@
     def take(q):
         for t in range(CHUNK // 32):
             for u in range(32):
-                line = place_smem[q * (CHUNK // 32) + t, u] & (2 * DEVICES * CAP - 9)
+                line = place_smem[q * (CHUNK // 32) + t, u]
                 rows_ref[t * 4 + u // 8, pl.ds(u % 8, 2, 8), :] = recv_ref[pl.ds(line, 2, 8), :]
 
     def finish(q, rows):

time: 59.3 us -> 59.2 us (level)
  no operation moved by 1% of the time
where the time goes in v6:
time: 59.2 us; the launch traced here: 59 us
  Pallas kernels  57.3 us (97%)
  local copies, waits for them, and re-layouts  0.98 us (2%)
  other arithmetic  0.7 us (1%)
    pallas_call x1, Pallas kernels, exchange(): pl.pallas_call(main_kernel, out_shape=jax.ShapeDtypeStruct((ROWS_DEV, PIV...  57.3 us

profile of v6, /device:TPU:1, one launch (start us, length us, event | category | flops | bytes accessed | tf_op | source)
XLA Modules:
  0.0 59.0 jit_solution(6225812209794275181)
XLA Ops:
  0.0 0.7 %pad_add_fusion = s32[1280]{0:T(1024)S(1)} fusion(s32[1024]{0:T(1024)} %param.7, s32[256]{0:T(256)} %param.5), kind=kLoop, calls=%fused_computation | loop fusion | flops 1280 | bytes 10240 | tf_op jit(solution)/shard_map/concatenate | solution.py:469
  0.7 57.3 %exchange.1 = f32[1024,256]{1,0:T(8,128)S(1)} custom-call(s32[1,1280]{1,0:T(1,128)S(1)} %reshape.3.index_ref, f32[1024,256]{1,0:T(8,128)} %ints_hbm.1, f32[1024,1024]{1,0:T(8,128)} %vec_hbm.1), custom_call_target="tpu_custom_call" | custom-call | tf_op jit(solution)/shard_map/exchange/pallas_call | solution.py:427
  58.1 1.0 %copy.6 = f32[1024,256]{1,0:T(8,128)} copy(f32[1024,256]{1,0:T(8,128)S(1)} %exchange.1) | data formatting | bytes 2097152
  (1 shorter events, 0.0 us)
